TPU v7x, 32 devices: a whole 2x2x4 slice. The times are simulated.
32 devices in a mesh: row: 8 (over y, x, core), col: 4 (over z).
Axes of the slice: x: 2, y: 2, z: 4, core: 2. Of those that a mesh axis runs over, the one named last changes fastest.
Arguments:
- tile_values: bfloat16 [8, 4, 64, 128, 128], P('row', 'col'), may hold values from -0.0625 to 0.0625
- tile_row: int32 [8, 4, 64], P('row', 'col'), may hold values from 0 to 3
- tile_col: int32 [8, 4, 64], P('row', 'col'), may hold values from 0 to 3
- tile_count: int32 [8, 4], P('row', 'col'), may hold values from 16 to 64, as said below
- primal_init: float32 [64, 2048], P(None, ('row', 'col')), may hold values from -3 to 3
- dual_init: float32 [64, 4096], P(None, ('row', 'col')), may hold values from -3 to 3
- cost_vector: float32 [2048], P(('row', 'col')), may hold values from -4 to 4
- lower_bound: float32 [2048], P(('row', 'col')), may hold values from -1 to -0.2
- upper_bound: float32 [2048], P(('row', 'col')), may hold values from 0.2 to 1
- bound_kind: int32 [2048], P(('row', 'col')), may hold values from 0 to 2
- row_kind: int32 [4096], P(('row', 'col')), may hold values from 0 to 1
- demand: float32 [64, 4096], P(None, ('row', 'col')), may hold values from -20 to 20
Outputs:
- primal_out: float32 [64, 2048], P(None, ('row', 'col'))
- dual_out: float32 [64, 4096], P(None, ('row', 'col'))
- residual_norm: float32 [3, 64], replicated
Inputs may be any that keep to these rules, and one draw needn't show every extreme that they name: `tile_count`: live tile slots of one device; some device has all 64 slots live.
All inputs are finite; a program needn't handle non-finite values.
Results may differ from a plain program's by a relative error of at most 0.0022.
Values may be sent and summed in bfloat16 or wider, within the bound.
A program may use at most 64 MiB of HBM per device.

v0:
```python
import jax
import jax.numpy as jnp
from jax import lax
from jax.sharding import PartitionSpec as P

ITERS = 3
PRIMAL_STEP = 0.4
DUAL_STEP = 0.4
NORM_EPS = 1e-06


def block_sum(onehot, product):
    return jnp.einsum("tr,sti->sri", onehot, product, precision=lax.Precision.HIGHEST)


def shards(
    tile_values,
    tile_row,
    tile_col,
    tile_count,
    primal_init,
    dual_init,
    cost_vector,
    lower_bound,
    upper_bound,
    bound_kind,
    row_kind,
    demand,
):
    blocks = tile_values[0, 0]
    slot_rows = tile_row[0, 0]
    slot_cols = tile_col[0, 0]
    live_count = tile_count[0, 0]
    slots = blocks.shape[0]
    tile_size = blocks.shape[-1]
    scenarios = primal_init.shape[0]
    row_devices = lax.axis_size("row")
    col_devices = lax.axis_size("col")
    col_blocks = row_devices // 2
    live_mask = jnp.arange(slots, dtype=jnp.int32) < live_count
    row_onehot = (
        (slot_rows[:, None] == jnp.arange(col_devices, dtype=jnp.int32)[None, :])
        & live_mask[:, None]
    ).astype(jnp.float32)
    col_onehot = (
        (slot_cols[:, None] == jnp.arange(col_blocks, dtype=jnp.int32)[None, :])
        & live_mask[:, None]
    ).astype(jnp.float32)
    total_rows = row_devices * col_devices * tile_size
    inequality = (row_kind == 1).astype(jnp.float32)
    primal = primal_init
    dual = dual_init
    partial_norms = []
    for iteration in range(ITERS):
        dual_half = lax.all_gather(dual.astype(jnp.bfloat16), "col", axis=1, tiled=True)
        grouped = dual_half.reshape(scenarios, col_devices, tile_size)
        picked = jnp.take(grouped, slot_rows, axis=1)
        product = jnp.einsum("tij,sti->stj", blocks, picked, preferred_element_type=jnp.float32)
        summed = block_sum(col_onehot, product)
        summed = summed.reshape(scenarios, col_blocks * tile_size)
        transposed = lax.psum_scatter(summed, "row", scatter_dimension=1, tiled=True)
        primal_next = primal - PRIMAL_STEP * (cost_vector[None, :] - transposed)
        primal_next = jnp.where(
            (bound_kind <= 1)[None, :], jnp.maximum(primal_next, lower_bound[None, :]), primal_next
        )
        primal_next = jnp.where(
            (bound_kind == 0)[None, :], jnp.minimum(primal_next, upper_bound[None, :]), primal_next
        )
        extrapolated = (2.0 * primal_next - primal).astype(jnp.bfloat16)
        gathered = lax.all_gather(extrapolated, "row", axis=1, tiled=True)
        apply_grouped = gathered.reshape(scenarios, col_blocks, tile_size)
        apply_picked = jnp.take(apply_grouped, slot_cols, axis=1)
        apply_product = jnp.einsum(
            "tij,stj->sti", blocks, apply_picked, preferred_element_type=jnp.float32
        )
        apply_summed = block_sum(row_onehot, apply_product)
        partial_value = apply_summed.reshape(scenarios, col_devices * tile_size)
        image = lax.psum_scatter(partial_value, "col", scatter_dimension=1, tiled=True)
        gap_rows = demand - image
        dual = dual + DUAL_STEP * gap_rows
        dual = jnp.where(inequality[None, :] > 0.0, jnp.maximum(dual, 0.0), dual)
        primal = primal_next
        squares = jnp.sum(gap_rows * gap_rows, axis=1)
        partial_norms.append(lax.psum(squares, ("row", "col")))
    totals = jnp.stack(partial_norms)
    residual_norm = jnp.sqrt(totals / total_rows + NORM_EPS)
    return (primal, dual, residual_norm)


def solution(mesh):
    return jax.shard_map(
        shards,
        mesh=mesh,
        in_specs=(
            P("row", "col", None, None, None),
            P("row", "col", None),
            P("row", "col", None),
            P("row", "col"),
            P(None, ("row", "col")),
            P(None, ("row", "col")),
            P(("row", "col")),
            P(("row", "col")),
            P(("row", "col")),
            P(("row", "col")),
            P(("row", "col")),
            P(None, ("row", "col")),
        ),
        out_specs=(P(None, ("row", "col")), P(None, ("row", "col")), P()),
        check_vma=False,
    )
```

profile of v0, /device:TPU:10, one launch (start us, length us, event | category | flops | bytes accessed | tf_op | source)
XLA Modules:
  0.0 312.5 jit_solution(8858715847128932885)
XLA Ops:
  7.2 0.8 compare_and_fusion.1
  8.0 0.7 compare_select_fusion.1
  9.4 0.8 convert_element_type.23
  10.1 12.3 %all_gather.18 = bf16[64,512]{1,0:T(8,128)(2,1)S(1)} all-gather(bf16[64,128]{1,0:T(8,128)(2,1)S(1)} %convert_element_type.23), channel_id=1, replica_groups=mesh['row'=8,'col'=4] {'col'}, dimensions={1}, use_global_device_ids=true | all-gather | bytes 81920 | tf_op jit(solution)/shard_map/all_gather | solution.py:55
  22.5 0.7 gather_fusion
  23.3 0.7 fusion.24
  24.1 2.0 fusion.42
  26.0 0.8 copy.57
  27.0 33.3 %reduce-scatter.19.cloned.1.call-done = f32[64,64]{1,0:T(8,128)} async-done(((f32[512,64]{1,0:T(8,128)}), f32[64,64]{1,0:T(8,128)}) %reduce-scatter.19.cloned.1.call-update) | async-done | bytes 16400
  60.3 0.8 copy.52
  61.3 8.3 %all_gather.19 = bf16[64,512]{0,1:T(8,128)(2,1)S(1)} all-gather(bf16[64,64]{0,1:T(8,128)(2,1)S(1)} %copy.29), channel_id=1, replica_groups=mesh['row'=8,'col'=4] {'row'}, dimensions={1}, use_global_device_ids=true | all-gather | bytes 73728 | tf_op jit(solution)/shard_map/all_gather | solution.py:70
  69.7 0.8 gather_fusion.1
  70.5 1.5 fusion.27
  72.1 2.0 fusion.20
  74.0 0.7 copy.92
  74.8 17.4 %reduce-scatter.13.cloned.1.call-done = f32[64,128]{1,0:T(8,128)} async-done(((f32[64,512]{1,0:T(8,128)}), f32[64,128]{1,0:T(8,128)}) %reduce-scatter.13.cloned.1.call-update) | async-done | bytes 32784 | tf_op jit(solution)/shard_map/reduce_scatter | solution.py:78
  92.2 0.8 fusion.75
  93.0 12.4 %all_gather.20 = bf16[64,512]{1,0:T(8,128)(2,1)S(1)} all-gather(bf16[64,128]{1,0:T(8,128)(2,1)S(1)} %fusion.75), channel_id=1, replica_groups=mesh['row'=8,'col'=4] {'col'}, dimensions={1}, use_global_device_ids=true | all-gather | bytes 81920 | tf_op jit(solution)/shard_map/all_gather | solution.py:55
  105.4 0.7 gather_fusion.2
  106.1 0.7 fusion.30
  106.9 2.0 fusion.45
  108.8 0.8 copy.58
  109.8 34.5 %reduce-scatter.21.cloned.1.call-done = f32[64,64]{1,0:T(8,128)} async-done(((f32[512,64]{1,0:T(8,128)}), f32[64,64]{1,0:T(8,128)}) %reduce-scatter.21.cloned.1.call-update) | async-done | bytes 16400
  144.2 0.8 copy.54
  145.2 8.5 %all_gather.21 = bf16[64,512]{0,1:T(8,128)(2,1)S(1)} all-gather(bf16[64,64]{0,1:T(8,128)(2,1)S(1)} %copy.35), channel_id=1, replica_groups=mesh['row'=8,'col'=4] {'row'}, dimensions={1}, use_global_device_ids=true | all-gather | bytes 73728 | tf_op jit(solution)/shard_map/all_gather | solution.py:70
  153.8 0.8 gather_fusion.3
  154.5 1.5 fusion.33
  156.1 2.0 fusion.16
  158.1 0.7 copy.91
  158.8 17.4 %reduce-scatter.15.cloned.1.call-done = f32[64,128]{1,0:T(8,128)} async-done(((f32[64,512]{1,0:T(8,128)}), f32[64,128]{1,0:T(8,128)}) %reduce-scatter.15.cloned.1.call-update) | async-done | bytes 32784 | tf_op jit(solution)/shard_map/reduce_scatter | solution.py:78
  176.2 0.8 fusion.95
  177.0 12.4 %all_gather.22 = bf16[64,512]{1,0:T(8,128)(2,1)S(1)} all-gather(bf16[64,128]{1,0:T(8,128)(2,1)S(1)} %fusion.95), channel_id=1, replica_groups=mesh['row'=8,'col'=4] {'col'}, dimensions={1}, use_global_device_ids=true | all-gather | bytes 81920 | tf_op jit(solution)/shard_map/all_gather | solution.py:55
  189.4 0.7 gather_fusion.4
  190.2 0.7 fusion.36
  190.9 2.0 fusion.48
  192.8 0.8 copy.59
  193.8 34.5 %reduce-scatter.23.cloned.1.call-done = f32[64,64]{1,0:T(8,128)} async-done(((f32[512,64]{1,0:T(8,128)}), f32[64,64]{1,0:T(8,128)}) %reduce-scatter.23.cloned.1.call-update) | async-done | bytes 16400
  228.2 0.8 copy.56
  229.0 0.7 subtract_convert_fusion
  229.8 8.3 %all_gather.23 = bf16[64,512]{0,1:T(8,128)(2,1)S(1)} all-gather(bf16[64,64]{0,1:T(8,128)(2,1)S(1)} %copy.41), channel_id=1, replica_groups=mesh['row'=8,'col'=4] {'row'}, dimensions={1}, use_global_device_ids=true | all-gather | bytes 73728 | tf_op jit(solution)/shard_map/all_gather | solution.py:70
  238.2 0.8 gather_fusion.5
  239.0 1.5 fusion.39
  240.5 2.0 fusion.12
  242.5 0.7 copy.90
  243.1 17.5 %reduce-scatter.17.cloned.1.call-done = f32[64,128]{1,0:T(8,128)} async-done(((f32[64,512]{1,0:T(8,128)}), f32[64,128]{1,0:T(8,128)}) %reduce-scatter.17.cloned.1.call-update) | async-done | bytes 32784 | tf_op jit(solution)/shard_map/reduce_scatter | solution.py:78
  260.6 1.5 multiply_reduce_fusion.2
  262.1 42.9 %all-reduce = (f32[1,64]{1,0:T(1,128)S(1)}, f32[1,64]{1,0:T(1,128)S(1)}, f32[1,64]{1,0:T(1,128)S(1)}) all-reduce(f32[1,64]{1,0:T(1,128)S(1)} %bitcast.152, f32[1,64]{1,0:T(1,128)S(1)} %bitcast.151, f32[1,64]{1,0:T(1,128)S(1)} %bitcast.150), channel_id=1, replica_groups=mesh['row'=8,'col'=4] {'row','col'}, use_global_device_ids=true, to_apply=%region_11.13 | all-reduce | flops 192 | bytes 1536 | tf_op jit(solution)/shard_map/psum | solution.py:84
  305.1 0.6 fusion.77
  (56 shorter events, 1.1 us)
Async XLA Ops:
  7.2 16.1 %copy-start = (bf16[1,1,64,128,128]{4,3,2,1,0:T(8,128)(2,1)S(1)}, bf16[1,1,64,128,128]{4,3,2,1,0:T(8,128)(2,1)}, u32[]{:S(2)}) copy-start(bf16[1,1,64,128,128]{4,3,2,1,0:T(8,128)(2,1)} %param.14) | copy-start | bytes 6291460
  7.2 53.1 %reduce-scatter.19.cloned.1.call-start = ((), (), s32[]{:S(2)}) async-start(), calls=%async_computation.9 | async-start | bytes 294912
  23.3 0.8 copy-start.9
  24.0 3.0 copy-start.11
  24.0 37.2 %copy-start.4 = (f32[64,64]{1,0:T(8,128)S(1)}, f32[64,64]{1,0:T(8,128)}, u32[]{:S(2)}) copy-start(f32[64,64]{1,0:T(8,128)} %param.18) | copy-start | bytes 49156
  24.0 37.1 %copy-start.6 = (f32[64]{0:T(128)S(1)}, f32[64]{0:T(128)}, u32[]{:S(2)}) copy-start(f32[64]{0:T(128)} %param.22) | copy-start | bytes 772
  24.0 37.1 %copy-start.7 = (f32[64]{0:T(128)S(1)}, f32[64]{0:T(128)}, u32[]{:S(2)}) copy-start(f32[64]{0:T(128)} %param.21) | copy-start | bytes 772
  24.0 37.1 %copy-start.8 = (f32[64]{0:T(128)S(1)}, f32[64]{0:T(128)}, u32[]{:S(2)}) copy-start(f32[64]{0:T(128)} %param.20) | copy-start | bytes 772
  26.9 65.3 %reduce-scatter.13.cloned.1.call-start = ((), (), s32[]{:S(2)}) async-start(), calls=%async_computation.6 | async-start | bytes 163840 | tf_op jit(solution)/shard_map/reduce_scatter | solution.py:78
  70.5 1.6 copy-start.10
  72.0 2.7 copy-start.12
  72.0 20.1 %copy-start.1 = (f32[64,128]{1,0:T(8,128)S(1)}, f32[64,128]{1,0:T(8,128)}, u32[]{:S(2)}) copy-start(f32[64,128]{1,0:T(8,128)} %param.19) | copy-start | bytes 98308
  72.1 20.1 %copy-start.2 = (f32[64,128]{1,0:T(8,128)S(1)}, f32[64,128]{1,0:T(8,128)}, u32[]{:S(2)}) copy-start(f32[64,128]{1,0:T(8,128)} %param.25) | copy-start | bytes 98308
  74.7 69.5 %reduce-scatter.21.cloned.1.call-start = ((), (), s32[]{:S(2)}) async-start(), calls=%async_computation.10 | async-start | bytes 294912
  109.7 66.5 %reduce-scatter.15.cloned.1.call-start = ((), (), s32[]{:S(2)}) async-start(), calls=%async_computation.7 | async-start | bytes 163840 | tf_op jit(solution)/shard_map/reduce_scatter | solution.py:78
  156.1 20.1 %copy-start.3 = (f32[64,128]{1,0:T(8,128)S(1)}, f32[64,128]{1,0:T(8,128)}, u32[]{:S(2)}) copy-start(f32[64,128]{1,0:T(8,128)} %reduce-scatter.13.cloned.1.call-done) | copy-start | bytes 98308
  158.7 69.5 %reduce-scatter.23.cloned.1.call-start = ((), (), s32[]{:S(2)}) async-start(), calls=%async_computation.11 | async-start | bytes 294912
  193.7 66.9 %reduce-scatter.17.cloned.1.call-start = ((), (), s32[]{:S(2)}) async-start(), calls=%async_computation.8 | async-start | bytes 163840 | tf_op jit(solution)/shard_map/reduce_scatter | solution.py:78
  240.5 20.1 %copy-start.5 = (f32[64,128]{1,0:T(8,128)S(1)}, f32[64,128]{1,0:T(8,128)}, u32[]{:S(2)}) copy-start(f32[64,128]{1,0:T(8,128)} %reduce-scatter.15.cloned.1.call-done) | copy-start | bytes 98308
Sparse Core Ops, SparseCore 0:
  27.0 33.2 reduce-scatter.18
  74.8 17.2 reduce-scatter.12
  109.8 34.3 reduce-scatter.20
  158.9 17.2 reduce-scatter.14
  193.8 34.3 reduce-scatter.22
  243.3 17.2 reduce-scatter.16
where the time goes:
time: 313 us
  waiting for transfers between devices  155 us (50%)
  blocking collectives  105 us (34%)
  matrix products  18.5 us (6%)
  between operations  15.1 us (5%)
  local copies, waits for them, and re-layouts  12.2 us (4%)
  other arithmetic  6.66 us (2%)
    unnamed x9, waiting for transfers between devices  102 us
    reduce_scatter x3, waiting for transfers between devices, shards(): lax.psum_scatter(partial_value, 'col', scatter_dimension=1, tiled=True)  52.2 us
    psum x1, blocking collectives, shards(): partial_norms.append(lax.psum(squares, ('row', 'col')))  42.9 us
    all_gather x3, blocking collectives, shards(): lax.all_gather(dual.astype(jnp.bfloat16), 'col', axis=1, tiled=True)  37.2 us
    all_gather x3, blocking collectives, shards(): gathered = lax.all_gather(extrapolated, 'row', axis=1, tiled=True)  25.1 us
    dot_general x6, matrix products, block_sum(): jnp.einsum('tr,sti->sri', onehot, product, precision=lax.Precision.HIGHEST)  11.8 us
    unnamed x35, local copies, waits for them, and re-layouts  7.05 us
  transfers between devices with their start and end apart: 6, of which 6 were waited for; matrix products, arithmetic and copies ran while one was open for 0% of the time, Pallas kernels for 0%

commit v1 on v0

--- a/solution.py
+++ b/solution.py
@@ -67,7 +67,31 @@
             (bound_kind == 0)[None, :], jnp.minimum(primal_next, upper_bound[None, :]), primal_next
         )
         extrapolated = (2.0 * primal_next - primal).astype(jnp.bfloat16)
-        gathered = lax.all_gather(extrapolated, "row", axis=1, tiled=True)
+        devices, index, extent = (
+            lax.axis_size("row"),
+            lax.axis_index("row"),
+            extrapolated.shape[1],
+        )
+        right = [(i, (i + 1) % devices) for i in range(devices)]
+        left = [(i, (i - 1) % devices) for i in range(devices)]
+        out = jnp.zeros(
+            (*extrapolated.shape[:1], devices * extent, *extrapolated.shape[1 + 1 :]),
+            extrapolated.dtype,
+        )
+        out = lax.dynamic_update_slice_in_dim(out, extrapolated, index * extent, axis=1)
+        from_left = from_right = extrapolated
+        half = devices // 2
+        for lap in range(1, half + 1):
+            from_left = lax.ppermute(from_left, "row", right)
+            out = lax.dynamic_update_slice_in_dim(
+                out, from_left, (index - lap) % devices * extent, axis=1
+            )
+            if lap < devices - half:
+                from_right = lax.ppermute(from_right, "row", left)
+                out = lax.dynamic_update_slice_in_dim(
+                    out, from_right, (index + lap) % devices * extent, axis=1
+                )
+        gathered = out
         apply_grouped = gathered.reshape(scenarios, col_blocks, tile_size)
         apply_picked = jnp.take(apply_grouped, slot_cols, axis=1)
         apply_product = jnp.einsum(

time: 313 us -> 335 us (1.070)
  blocking collectives: 105 us -> 80.5 us
  starting transfers between devices: 0.25 us -> 20.7 us
  waiting for transfers between devices: 155 us -> 174 us
  local copies, waits for them, and re-layouts: 12.2 us -> 18.1 us
    all_gather x3 -> x0, blocking collectives: 25.1 us -> none  [shards(): gathered = lax.all_gather(extrapolated, 'row', axis=1, tiled=True)]
    ppermute x0 -> x21, starting transfers between devices: none -> 20.5 us  [the longest x9 16.1 us: shards(): from_right = lax.ppermute(from_right, 'row', left)]
    ppermute x0 -> x21, waiting for transfers between devices: none -> 11.7 us  [the longest x12 11.6 us: shards(): from_left = lax.ppermute(from_left, 'row', right)]
    reduce_scatter x3, waiting for transfers between devices: 52.2 us -> 60.4 us  [shards(): lax.psum_scatter(partial_value, 'col', scatter_dimension=1, tiled=True)]
    dynamic_update_slice x0 -> x24, local copies, waits for them, and re-layouts: none -> 6.37 us  [the longest x12 3.15 us: shards(): lax.dynamic_update_slice_in_dim(out, from_left, (index - lap) % devices *...]
  transfers between devices with their start and end apart: 6 -> 27, of which waited for: 6 -> 15; matrix products, arithmetic and copies ran while one was open for 0% -> 2% of each run, Pallas kernels for 0% -> 0%
where the time goes in v1:
time: 335 us; the launch traced here: 334 us
  waiting for transfers between devices  174 us (52%)
  blocking collectives  80.5 us (24%)
  starting transfers between devices  20.7 us (6%)
  matrix products  18.6 us (6%)
  local copies, waits for them, and re-layouts  18.1 us (5%)
  between operations  15.4 us (5%)
  other arithmetic  6.66 us (2%)
    unnamed x9, waiting for transfers between devices  102 us
    reduce_scatter x3, waiting for transfers between devices, shards(): lax.psum_scatter(partial_value, 'col', scatter_dimension=1, tiled=True)  60.4 us
    psum x1, blocking collectives, shards(): partial_norms.append(lax.psum(squares, ('row', 'col')))  42.9 us
    all_gather x3, blocking collectives, shards(): lax.all_gather(dual.astype(jnp.bfloat16), 'col', axis=1, tiled=True)  37.6 us
    ppermute x9, starting transfers between devices, shards(): from_right = lax.ppermute(from_right, 'row', left)  16.1 us
    dot_general x6, matrix products, block_sum(): jnp.einsum('tr,sti->sri', onehot, product, precision=lax.Precision.HIGHEST)  11.8 us
    ppermute x12, waiting for transfers between devices, shards(): from_left = lax.ppermute(from_left, 'row', right)  11.6 us
    unnamed x35, local copies, waits for them, and re-layouts  7.09 us
  transfers between devices with their start and end apart: 27, of which 15 were waited for; matrix products, arithmetic and copies ran while one was open for 2% of the time, Pallas kernels for 0%

profile of v1, /device:TPU:10, one launch (start us, length us, event | category | flops | bytes accessed | tf_op | source)
XLA Modules:
  0.0 334.3 jit_solution(15706722744286478405)
XLA Ops:
  7.2 0.8 compare_select_fusion.1
  10.1 12.3 %all_gather.9 = bf16[64,512]{1,0:T(8,128)(2,1)S(1)} all-gather(bf16[64,128]{1,0:T(8,128)(2,1)S(1)} %convert_element_type.23), channel_id=1, replica_groups=mesh['row'=8,'col'=4] {'col'}, dimensions={1}, use_global_device_ids=true | all-gather | bytes 81920 | tf_op jit(solution)/shard_map/all_gather | solution.py:55
  24.1 2.0 fusion.42
  26.0 0.8 copy.45
  27.0 33.4 %reduce-scatter.19.cloned.1.call-done = f32[64,64]{1,0:T(8,128)} async-done(((f32[512,64]{1,0:T(8,128)}), f32[64,64]{1,0:T(8,128)}) %reduce-scatter.19.cloned.1.call-update) | async-done | bytes 16400
  60.3 0.8 copy.40
  61.3 1.7 collective-permute-start.1
  63.0 1.4 collective-permute-done
  64.5 1.7 collective-permute-start.3
  66.2 1.4 collective-permute-done.2
  67.8 1.9 collective-permute-start.5
  69.7 1.1 collective-permute-done.4
  70.8 1.2 collective-permute-start.6
  75.0 1.5 fusion.27
  76.6 2.0 fusion.20
  79.3 20.0 %reduce-scatter.13.cloned.1.call-done = f32[64,128]{1,0:T(8,128)} async-done(((f32[64,512]{1,0:T(8,128)}), f32[64,128]{1,0:T(8,128)}) %reduce-scatter.13.cloned.1.call-update) | async-done | bytes 32784 | tf_op jit(solution)/shard_map/reduce_scatter | solution.py:102
  100.2 12.6 %all_gather.10 = bf16[64,512]{1,0:T(8,128)(2,1)S(1)} all-gather(bf16[64,128]{1,0:T(8,128)(2,1)S(1)} %fusion.75), channel_id=1, replica_groups=mesh['row'=8,'col'=4] {'col'}, dimensions={1}, use_global_device_ids=true | all-gather | bytes 81920 | tf_op jit(solution)/shard_map/all_gather | solution.py:55
  114.3 2.0 fusion.45
  116.2 0.8 copy.46
  117.2 34.5 %reduce-scatter.21.cloned.1.call-done = f32[64,64]{1,0:T(8,128)} async-done(((f32[512,64]{1,0:T(8,128)}), f32[64,64]{1,0:T(8,128)}) %reduce-scatter.21.cloned.1.call-update) | async-done | bytes 16400
  151.6 0.8 copy.42
  152.6 1.7 collective-permute-start.8
  154.3 1.4 collective-permute-done.7
  155.7 1.7 collective-permute-start.10
  157.5 1.4 collective-permute-done.9
  159.1 1.9 collective-permute-start.12
  161.0 1.0 collective-permute-done.11
  162.0 1.2 collective-permute-start.13
  166.2 1.5 fusion.33
  167.8 2.0 fusion.16
  170.5 20.1 %reduce-scatter.15.cloned.1.call-done = f32[64,128]{1,0:T(8,128)} async-done(((f32[64,512]{1,0:T(8,128)}), f32[64,128]{1,0:T(8,128)}) %reduce-scatter.15.cloned.1.call-update) | async-done | bytes 32784 | tf_op jit(solution)/shard_map/reduce_scatter | solution.py:102
  191.4 12.6 %all_gather.11 = bf16[64,512]{1,0:T(8,128)(2,1)S(1)} all-gather(bf16[64,128]{1,0:T(8,128)(2,1)S(1)} %fusion.95), channel_id=1, replica_groups=mesh['row'=8,'col'=4] {'col'}, dimensions={1}, use_global_device_ids=true | all-gather | bytes 81920 | tf_op jit(solution)/shard_map/all_gather | solution.py:55
  205.5 2.0 fusion.48
  207.5 0.8 copy.47
  208.4 34.5 %reduce-scatter.23.cloned.1.call-done = f32[64,64]{1,0:T(8,128)} async-done(((f32[512,64]{1,0:T(8,128)}), f32[64,64]{1,0:T(8,128)}) %reduce-scatter.23.cloned.1.call-update) | async-done | bytes 16400
  242.9 0.8 copy.44
  244.4 1.7 collective-permute-start.15
  246.1 1.4 collective-permute-done.14
  247.5 1.7 collective-permute-start.17
  249.3 1.4 collective-permute-done.16
  250.9 1.9 collective-permute-start.19
  252.8 1.1 collective-permute-done.18
  253.8 1.2 collective-permute-start.20
  258.0 1.5 fusion.39
  259.6 2.0 fusion.12
  262.2 20.2 %reduce-scatter.17.cloned.1.call-done = f32[64,128]{1,0:T(8,128)} async-done(((f32[64,512]{1,0:T(8,128)}), f32[64,128]{1,0:T(8,128)}) %reduce-scatter.17.cloned.1.call-update) | async-done | bytes 32784 | tf_op jit(solution)/shard_map/reduce_scatter | solution.py:102
  282.4 1.5 multiply_reduce_fusion.2
  283.9 42.9 %all-reduce = (f32[1,64]{1,0:T(1,128)S(1)}, f32[1,64]{1,0:T(1,128)S(1)}, f32[1,64]{1,0:T(1,128)S(1)}) all-reduce(f32[1,64]{1,0:T(1,128)S(1)} %bitcast.161, f32[1,64]{1,0:T(1,128)S(1)} %bitcast.160, f32[1,64]{1,0:T(1,128)S(1)} %bitcast.159), channel_id=1, replica_groups=mesh['row'=8,'col'=4] {'row','col'}, use_global_device_ids=true, to_apply=%region_11.13 | all-reduce | flops 192 | bytes 1536 | tf_op jit(solution)/shard_map/psum | solution.py:108
  (119 shorter events, 20.7 us)
Async XLA Ops:
  7.2 16.1 %copy-start = (bf16[1,1,64,128,128]{4,3,2,1,0:T(8,128)(2,1)S(1)}, bf16[1,1,64,128,128]{4,3,2,1,0:T(8,128)(2,1)}, u32[]{:S(2)}) copy-start(bf16[1,1,64,128,128]{4,3,2,1,0:T(8,128)(2,1)} %param.14) | copy-start | bytes 6291460
  7.2 53.2 %reduce-scatter.19.cloned.1.call-start = ((), (), s32[]{:S(2)}) async-start(), calls=%async_computation.9 | async-start | bytes 294912
  23.3 0.8 copy-start.9
  24.0 3.0 copy-start.11
  24.0 37.2 %copy-start.4 = (f32[64,64]{1,0:T(8,128)S(1)}, f32[64,64]{1,0:T(8,128)}, u32[]{:S(2)}) copy-start(f32[64,64]{1,0:T(8,128)} %param.18) | copy-start | bytes 49156
  24.0 37.2 %copy-start.6 = (f32[64]{0:T(128)S(1)}, f32[64]{0:T(128)}, u32[]{:S(2)}) copy-start(f32[64]{0:T(128)} %param.22) | copy-start | bytes 772
  24.0 37.2 %copy-start.7 = (f32[64]{0:T(128)S(1)}, f32[64]{0:T(128)}, u32[]{:S(2)}) copy-start(f32[64]{0:T(128)} %param.21) | copy-start | bytes 772
  24.0 37.1 %copy-start.8 = (f32[64]{0:T(128)S(1)}, f32[64]{0:T(128)}, u32[]{:S(2)}) copy-start(f32[64]{0:T(128)} %param.20) | copy-start | bytes 772
  26.9 72.5 %reduce-scatter.13.cloned.1.call-start = ((), (), s32[]{:S(2)}) async-start(), calls=%async_computation.6 | async-start | bytes 163840 | tf_op jit(solution)/shard_map/reduce_scatter | solution.py:102
  61.2 3.2 collective-permute-start
  61.3 3.2 collective-permute-start.1
  64.4 3.2 collective-permute-start.2
  64.5 3.4 %collective-permute-start.3 = (bf16[64,64]{1,0:T(8,128)(2,1)S(1)}, bf16[64,64]{1,0:T(8,128)(2,1)S(1)}, u32[]{:S(2)}, u32[]{:S(2)}) collective-permute-start(bf16[64,64]{1,0:T(8,128)(2,1)S(1)} %collective-permute-done.1), channel_id=1, source_target_pairs={{0,28},{4,0},{8,4},{12,8},{16,12},{20,16},{24,20},{28,24},{1,29},{... | collective-permute-start | bytes 24584 | tf_op jit(solution)/shard_map/ppermute | solution.py:90
  67.6 3.2 collective-permute-start.4
  67.8 5.8 %collective-permute-start.5 = (bf16[64,64]{1,0:T(8,128)(2,1)S(1)}, bf16[64,64]{1,0:T(8,128)(2,1)S(1)}, u32[]{:S(2)}, u32[]{:S(2)}) collective-permute-start(bf16[64,64]{1,0:T(8,128)(2,1)S(1)} %collective-permute-done.3), channel_id=1, source_target_pairs={{0,28},{4,0},{8,4},{12,8},{16,12},{20,16},{24,20},{28,24},{1,29},{... | collective-permute-start | bytes 24584 | tf_op jit(solution)/shard_map/ppermute | solution.py:90
  70.8 3.3 collective-permute-start.6
  75.0 1.6 copy-start.10
  76.6 2.7 copy-start.12
  76.6 22.8 %copy-start.1 = (f32[64,128]{1,0:T(8,128)S(1)}, f32[64,128]{1,0:T(8,128)}, u32[]{:S(2)}) copy-start(f32[64,128]{1,0:T(8,128)} %param.19) | copy-start | bytes 98308
  76.6 22.8 %copy-start.2 = (f32[64,128]{1,0:T(8,128)S(1)}, f32[64,128]{1,0:T(8,128)}, u32[]{:S(2)}) copy-start(f32[64,128]{1,0:T(8,128)} %param.25) | copy-start | bytes 98308
  79.3 72.4 %reduce-scatter.21.cloned.1.call-start = ((), (), s32[]{:S(2)}) async-start(), calls=%async_computation.10 | async-start | bytes 294912
  117.1 73.5 %reduce-scatter.15.cloned.1.call-start = ((), (), s32[]{:S(2)}) async-start(), calls=%async_computation.7 | async-start | bytes 163840 | tf_op jit(solution)/shard_map/reduce_scatter | solution.py:102
  152.5 3.2 collective-permute-start.7
  152.6 3.2 collective-permute-start.8
  155.7 3.2 collective-permute-start.9
  155.7 3.4 %collective-permute-start.10 = (bf16[64,64]{1,0:T(8,128)(2,1)S(1)}, bf16[64,64]{1,0:T(8,128)(2,1)S(1)}, u32[]{:S(2)}, u32[]{:S(2)}) collective-permute-start(bf16[64,64]{1,0:T(8,128)(2,1)S(1)} %collective-permute-done.8), channel_id=1, source_target_pairs={{0,28},{4,0},{8,4},{12,8},{16,12},{20,16},{24,20},{28,24},{1,29},{... | collective-permute-start | bytes 24584 | tf_op jit(solution)/shard_map/ppermute | solution.py:90
  158.9 3.2 collective-permute-start.11
  159.1 5.8 %collective-permute-start.12 = (bf16[64,64]{1,0:T(8,128)(2,1)S(1)}, bf16[64,64]{1,0:T(8,128)(2,1)S(1)}, u32[]{:S(2)}, u32[]{:S(2)}) collective-permute-start(bf16[64,64]{1,0:T(8,128)(2,1)S(1)} %collective-permute-done.10), channel_id=1, source_target_pairs={{0,28},{4,0},{8,4},{12,8},{16,12},{20,16},{24,20},{28,24},{1,29},{... | collective-permute-start | bytes 24584 | tf_op jit(solution)/shard_map/ppermute | solution.py:90
  162.0 3.2 collective-permute-start.13
  167.8 22.9 %copy-start.3 = (f32[64,128]{1,0:T(8,128)S(1)}, f32[64,128]{1,0:T(8,128)}, u32[]{:S(2)}) copy-start(f32[64,128]{1,0:T(8,128)} %reduce-scatter.13.cloned.1.call-done) | copy-start | bytes 98308
  170.4 72.4 %reduce-scatter.23.cloned.1.call-start = ((), (), s32[]{:S(2)}) async-start(), calls=%async_computation.11 | async-start | bytes 294912
  208.4 74.1 %reduce-scatter.17.cloned.1.call-start = ((), (), s32[]{:S(2)}) async-start(), calls=%async_computation.8 | async-start | bytes 163840 | tf_op jit(solution)/shard_map/reduce_scatter | solution.py:102
  244.3 3.2 collective-permute-start.14
  244.4 3.2 collective-permute-start.15
  247.5 3.2 collective-permute-start.16
  247.5 3.3 collective-permute-start.17
  250.7 3.2 collective-permute-start.18
  250.9 5.8 %collective-permute-start.19 = (bf16[64,64]{1,0:T(8,128)(2,1)S(1)}, bf16[64,64]{1,0:T(8,128)(2,1)S(1)}, u32[]{:S(2)}, u32[]{:S(2)}) collective-permute-start(bf16[64,64]{1,0:T(8,128)(2,1)S(1)} %collective-permute-done.17), channel_id=1, source_target_pairs={{0,28},{4,0},{8,4},{12,8},{16,12},{20,16},{24,20},{28,24},{1,29},{... | collective-permute-start | bytes 24584 | tf_op jit(solution)/shard_map/ppermute | solution.py:90
  253.8 3.2 collective-permute-start.20
  259.6 22.8 %copy-start.5 = (f32[64,128]{1,0:T(8,128)S(1)}, f32[64,128]{1,0:T(8,128)}, u32[]{:S(2)}) copy-start(f32[64,128]{1,0:T(8,128)} %reduce-scatter.15.cloned.1.call-done) | copy-start | bytes 98308
Sparse Core Ops, SparseCore 0:
  27.0 33.2 reduce-scatter.18
  79.4 19.9 reduce-scatter.12
  117.2 34.3 reduce-scatter.20
  170.6 20.0 reduce-scatter.14
  208.5 34.3 reduce-scatter.22
  262.4 20.0 reduce-scatter.16
